TPU v7x, 32 devices: a whole 2x2x4 slice. The times are simulated.
32 devices in a mesh: fsdp: 4 (over z), ctx: 4 (over y, x), tp: 2 (over core).
Axes of the slice: x: 2, y: 2, z: 4, core: 2. Of those that a mesh axis runs over, the one named last changes fastest.
Arguments:
- hidden_in: bfloat16 [16, 1024, 768], P('fsdp', 'ctx'), may hold values from -6 to 6
- lengths: int32 [16], P('fsdp'), may hold values from 256 to 1024, as said below
- out_grad: bfloat16 [16, 1024, 768], P('fsdp', 'ctx'), may hold values from -6 to 6
- w_qkv: bfloat16 [3, 768, 768], P(None, 'fsdp', 'tp'), may hold values from -0.21875 to 0.21875
- qv_bias: bfloat16 [2, 12, 64], P(None, 'tp', 'fsdp'), may hold values from -0.3125 to 0.3125
- w_out: bfloat16 [768, 768], P('tp', 'fsdp'), may hold values from -3.5 to 3.5
- out_biases: bfloat16 [2, 768], P(None, 'fsdp'), may hold values from -4 to 4
- norm_gains: bfloat16 [2, 768], P(None, 'fsdp'), may hold values from 0.25 to 1.75
- norm_biases: bfloat16 [2, 768], P(None, 'fsdp'), may hold values from -4 to 4
- w_in: bfloat16 [768, 3072], P(None, ('fsdp', 'tp')), may hold values from -0.21875 to 0.21875
- ffn_bias: bfloat16 [3072], P(('fsdp', 'tp')), may hold values from -6 to 6
- w_ffo: bfloat16 [3072, 768], P(('fsdp', 'tp')), may hold values from -0.109375 to 0.109375
Outputs:
- hidden_out: bfloat16 [16, 1024, 768], P('fsdp', 'ctx')
- hidden_grad: bfloat16 [16, 1024, 768], P('fsdp', 'ctx')
- grad_qkv: float32 [3, 768, 768], P(None, 'fsdp', 'tp')
- grad_qv_bias: float32 [2, 12, 64], P(None, 'tp', 'fsdp')
- grad_out: float32 [768, 768], P('tp', 'fsdp')
- grad_out_biases: float32 [2, 768], P(None, 'fsdp')
- grad_gains: float32 [2, 768], P(None, 'fsdp')
- grad_shifts: float32 [2, 768], P(None, 'fsdp')
- grad_in: float32 [768, 3072], P(None, ('fsdp', 'tp'))
- grad_ffn_bias: float32 [3072], P(('fsdp', 'tp'))
- grad_ffo: float32 [3072, 768], P(('fsdp', 'tp'))
Inputs may be any that keep to these rules, and one draw needn't show every extreme that they name: lengths[s] counts the valid positions of slot s from its start; in every draw one slot has 1024 and one has 256.
All inputs are finite; a program needn't handle non-finite values.
Results may differ from a plain program's by a relative error of at most 0.019.
Values may be sent and summed in bfloat16 or wider, within the bound.
A program may use at most 192 MiB of HBM per device.

v0:
```python
import jax
import jax.numpy as jnp
from jax import lax
from jax.sharding import PartitionSpec as P

epsilon = 1e-05
masked_value = -1e30
heads_together = 2


def norm_rows(residual, gain_row, shift_row):
    centre = jnp.mean(residual, axis=-1, keepdims=True)
    centred = residual - centre
    spread = jnp.mean(centred * centred, axis=-1, keepdims=True)
    return centred * lax.rsqrt(spread + epsilon) * gain_row + shift_row


def gelu_exact(values):
    return jax.nn.gelu(values, approximate=False)


def split_heads(matrix, head_dim):
    return matrix.reshape(matrix.shape[0], matrix.shape[1] // head_dim, head_dim)


def block_scores(query_heads, key_heads, key_mask, score_scale):
    scores = (
        jnp.einsum("qhd,khd->hqk", query_heads, key_heads, preferred_element_type=jnp.float32)
        * score_scale
    )
    return jnp.where(key_mask[None, None, :], scores, masked_value)


def attend_slot(queries, key_value, length, score_scale, head_dim):
    gathered = lax.all_gather(key_value, "ctx", axis=1, tiled=True)
    seq_len = gathered.shape[1]
    key_mask = lax.iota(jnp.int32, seq_len) < length
    block_width = heads_together * head_dim
    outputs = []
    totals = []
    for head_block in range(queries.shape[1] // block_width):
        columns = slice(head_block * block_width, (head_block + 1) * block_width)
        query_heads = split_heads(queries[:, columns], head_dim)
        key_heads = split_heads(gathered[0][:, columns], head_dim)
        value_heads = split_heads(gathered[1][:, columns], head_dim)
        scores = block_scores(query_heads, key_heads, key_mask, score_scale)
        highest = jnp.max(scores, axis=-1, keepdims=True)
        log_total = highest + jnp.log(jnp.sum(jnp.exp(scores - highest), axis=-1, keepdims=True))
        weights_low = jnp.exp(scores - log_total).astype(jnp.bfloat16)
        attended = jnp.einsum(
            "hqk,khd->qhd", weights_low, value_heads, preferred_element_type=jnp.float32
        )
        outputs.append(attended.reshape(attended.shape[0], block_width))
        totals.append(log_total[:, :, 0])
    return (jnp.concatenate(outputs, axis=1).astype(jnp.bfloat16), jnp.concatenate(totals, axis=0))


def slot_grads(queries, key_value, length, grad_mixed, log_totals, score_scale, head_dim):
    gathered = lax.all_gather(key_value, "ctx", axis=1, tiled=True)
    seq_len = gathered.shape[1]
    key_mask = lax.iota(jnp.int32, seq_len) < length
    block_width = heads_together * head_dim
    query_grads = []
    key_grads = []
    value_grads = []
    inner_parts = []
    for head_block in range(queries.shape[1] // block_width):
        columns = slice(head_block * block_width, (head_block + 1) * block_width)
        heads_range = slice(head_block * heads_together, (head_block + 1) * heads_together)
        query_heads = split_heads(queries[:, columns], head_dim)
        key_heads = split_heads(gathered[0][:, columns], head_dim)
        value_heads = split_heads(gathered[1][:, columns], head_dim)
        grad_heads = split_heads(grad_mixed[:, columns], head_dim)
        scores = block_scores(query_heads, key_heads, key_mask, score_scale)
        softmax_rows = jnp.exp(scores - log_totals[heads_range, :, None])
        grad_weights = jnp.einsum(
            "qhd,khd->hqk", grad_heads, value_heads, preferred_element_type=jnp.float32
        )
        inner_sums = jnp.sum(softmax_rows * grad_weights, axis=-1)
        grad_scores = (softmax_rows * (grad_weights - inner_sums[:, :, None])).astype(jnp.bfloat16)
        grad_query = (
            jnp.einsum("hqk,khd->qhd", grad_scores, key_heads, preferred_element_type=jnp.float32)
            * score_scale
        )
        query_grads.append(grad_query.reshape(grad_query.shape[0], block_width))
        inner_parts.append(inner_sums)
        grad_key = (
            jnp.einsum("hqk,qhd->khd", grad_scores, query_heads, preferred_element_type=jnp.float32)
            * score_scale
        )
        grad_value = jnp.einsum(
            "hqk,qhd->khd",
            softmax_rows.astype(jnp.bfloat16),
            grad_heads,
            preferred_element_type=jnp.float32,
        )
        key_grads.append(grad_key.reshape(seq_len, block_width))
        value_grads.append(grad_value.reshape(seq_len, block_width))
    grad_queries = jnp.concatenate(query_grads, axis=1)
    key_terms = jnp.stack(
        [jnp.concatenate(key_grads, axis=1), jnp.concatenate(value_grads, axis=1)]
    )
    own_grads = lax.psum_scatter(
        key_terms.astype(jnp.bfloat16), "ctx", scatter_dimension=1, tiled=True
    ).astype(jnp.float32)
    return (grad_queries, own_grads)


def per_device(
    hidden_in,
    lengths,
    out_grad,
    w_qkv,
    qv_bias,
    w_out,
    out_biases,
    norm_gains,
    norm_biases,
    w_in,
    ffn_bias,
    w_ffo,
):
    w_proj, proj_bias, w_back, branch_biases, gains, shifts, w_up, up_bias, w_down = (
        lax.all_gather(w_qkv, "fsdp", axis=1, tiled=True),
        lax.all_gather(qv_bias, "fsdp", axis=2, tiled=True),
        lax.all_gather(w_out, "fsdp", axis=1, tiled=True),
        lax.all_gather(out_biases, "fsdp", axis=1, tiled=True),
        lax.all_gather(norm_gains, "fsdp", axis=1, tiled=True),
        lax.all_gather(norm_biases, "fsdp", axis=1, tiled=True),
        lax.all_gather(w_in, "fsdp", axis=1, tiled=True),
        lax.all_gather(ffn_bias, "fsdp", axis=0, tiled=True),
        lax.all_gather(w_ffo, "fsdp", axis=0, tiled=True),
    )
    slot_count, block_len, model_width = hidden_in.shape
    token_count = slot_count * block_len
    head_dim = proj_bias.shape[2]
    score_scale = head_dim ** (-0.5)
    local_width = w_proj.shape[2]
    contract_rows = (((0,), (0,)), ((), ()))
    contract_cols = (((1,), (1,)), ((), ()))
    bias_table = jnp.stack(
        [
            proj_bias[0].reshape(local_width).astype(jnp.float32),
            jnp.zeros((local_width,), jnp.float32),
            proj_bias[1].reshape(local_width).astype(jnp.float32),
        ]
    )
    projected = (
        jnp.einsum("sbd,pdc->spbc", hidden_in, w_proj, preferred_element_type=jnp.float32)
        + bias_table[None, :, None, :]
    ).astype(jnp.bfloat16)
    queries = projected[:, 0]
    key_values = projected[:, 1:]
    attended, log_totals = lax.map(
        lambda slot_items: attend_slot(
            slot_items[0], slot_items[1], slot_items[2], score_scale, head_dim
        ),
        (queries, key_values, lengths),
    )
    mixed_rows = attended.reshape(token_count, local_width)
    token_rows = hidden_in.reshape(token_count, model_width)
    branch = lax.psum(
        jnp.dot(mixed_rows, w_back, preferred_element_type=jnp.float32), "tp"
    ) + branch_biases[0].astype(jnp.float32)
    first_norm, first_pull = jax.vjp(
        norm_rows,
        token_rows.astype(jnp.float32) + branch,
        gains[0].astype(jnp.float32),
        shifts[0].astype(jnp.float32),
    )
    first_low = first_norm.astype(jnp.bfloat16)
    hidden_pre = jnp.dot(first_low, w_up, preferred_element_type=jnp.float32) + up_bias.astype(
        jnp.float32
    )
    activated, gelu_pull = jax.vjp(gelu_exact, hidden_pre)
    activated_low = activated.astype(jnp.bfloat16)
    second_branch = lax.psum(
        jnp.dot(activated_low, w_down, preferred_element_type=jnp.float32), "tp"
    ) + branch_biases[1].astype(jnp.float32)
    output_rows, second_pull = jax.vjp(
        norm_rows,
        first_norm + second_branch,
        gains[1].astype(jnp.float32),
        shifts[1].astype(jnp.float32),
    )
    hidden_out = output_rows.astype(jnp.bfloat16).reshape(slot_count, block_len, model_width)
    own_start = lax.axis_index("ctx") * block_len
    positions = own_start + lax.iota(jnp.int32, block_len)
    row_mask = (positions[None, :] < lengths[:, None]).astype(jnp.float32).reshape(token_count, 1)
    grad_output = out_grad.reshape(token_count, model_width).astype(jnp.float32) * row_mask
    grad_second, grad_gain_two, grad_shift_two = second_pull(grad_output)
    grad_second_low = grad_second.astype(jnp.bfloat16)
    grad_down = lax.dot_general(
        activated_low, grad_second_low, contract_rows, preferred_element_type=jnp.float32
    )
    grad_act = lax.dot_general(
        grad_second_low, w_down, contract_cols, preferred_element_type=jnp.float32
    )
    (grad_pre,) = gelu_pull(grad_act)
    grad_pre_low = grad_pre.astype(jnp.bfloat16)
    grad_up = lax.dot_general(
        first_low, grad_pre_low, contract_rows, preferred_element_type=jnp.float32
    )
    grad_first = grad_second + lax.psum(
        lax.dot_general(grad_pre_low, w_up, contract_cols, preferred_element_type=jnp.float32), "tp"
    )
    grad_resid, grad_gain_one, grad_shift_one = first_pull(grad_first)
    grad_branch_low = grad_resid.astype(jnp.bfloat16)
    grad_back = lax.dot_general(
        mixed_rows, grad_branch_low, contract_rows, preferred_element_type=jnp.float32
    )
    grad_mixed = (
        lax.dot_general(grad_branch_low, w_back, contract_cols, preferred_element_type=jnp.float32)
        .astype(jnp.bfloat16)
        .reshape(slot_count, block_len, local_width)
    )
    grad_queries, grad_pairs = lax.map(
        lambda slot_items: slot_grads(
            slot_items[0],
            slot_items[1],
            slot_items[2],
            slot_items[3],
            slot_items[4],
            score_scale,
            head_dim,
        ),
        (queries, key_values, lengths, grad_mixed, log_totals),
    )
    grad_proj = jnp.concatenate(
        [grad_queries.astype(jnp.bfloat16)[:, None], grad_pairs.astype(jnp.bfloat16)], axis=1
    )
    grad_w_proj = jnp.einsum(
        "sbd,spbc->pdc", hidden_in, grad_proj, preferred_element_type=jnp.float32
    )
    grad_proj_bias = jnp.stack(
        [
            jnp.sum(grad_proj[:, 0], axis=(0, 1), dtype=jnp.float32),
            jnp.sum(grad_proj[:, 2], axis=(0, 1), dtype=jnp.float32),
        ]
    ).reshape(proj_bias.shape)
    grad_tokens = jnp.einsum(
        "spbc,pdc->sbd", grad_proj, w_proj, preferred_element_type=jnp.float32
    ).reshape(token_count, model_width)
    hidden_grad = (
        (grad_resid + lax.psum(grad_tokens.astype(jnp.bfloat16), "tp").astype(jnp.float32))
        .astype(jnp.bfloat16)
        .reshape(slot_count, block_len, model_width)
    )
    grad_biases = jnp.stack(
        [
            jnp.sum(grad_branch_low, axis=0, dtype=jnp.float32),
            jnp.sum(grad_second_low, axis=0, dtype=jnp.float32),
        ]
    )
    grad_gains = jnp.stack([grad_gain_one, grad_gain_two])
    grad_shifts = jnp.stack([grad_shift_one, grad_shift_two])
    grad_up_bias = jnp.sum(grad_pre_low, axis=0, dtype=jnp.float32)
    shares = (
        lax.psum_scatter(
            grad_w_proj.astype(jnp.bfloat16), "fsdp", scatter_dimension=1, tiled=True
        ).astype(jnp.float32),
        lax.psum_scatter(
            grad_proj_bias.astype(jnp.bfloat16), "fsdp", scatter_dimension=2, tiled=True
        ).astype(jnp.float32),
        lax.psum_scatter(
            grad_back.astype(jnp.bfloat16), "fsdp", scatter_dimension=1, tiled=True
        ).astype(jnp.float32),
        lax.psum_scatter(
            grad_biases.astype(jnp.bfloat16), "fsdp", scatter_dimension=1, tiled=True
        ).astype(jnp.float32),
        lax.psum_scatter(
            grad_gains.astype(jnp.bfloat16), "fsdp", scatter_dimension=1, tiled=True
        ).astype(jnp.float32),
        lax.psum_scatter(
            grad_shifts.astype(jnp.bfloat16), "fsdp", scatter_dimension=1, tiled=True
        ).astype(jnp.float32),
        lax.psum_scatter(
            grad_up.astype(jnp.bfloat16), "fsdp", scatter_dimension=1, tiled=True
        ).astype(jnp.float32),
        lax.psum_scatter(
            grad_up_bias.astype(jnp.bfloat16), "fsdp", scatter_dimension=0, tiled=True
        ).astype(jnp.float32),
        lax.psum_scatter(
            grad_down.astype(jnp.bfloat16), "fsdp", scatter_dimension=0, tiled=True
        ).astype(jnp.float32),
    )
    owned = (
        lax.psum(shares[0].astype(jnp.bfloat16), "ctx").astype(jnp.float32),
        lax.psum(shares[1].astype(jnp.bfloat16), "ctx").astype(jnp.float32),
        lax.psum(shares[2].astype(jnp.bfloat16), "ctx").astype(jnp.float32),
        lax.psum(shares[3].astype(jnp.bfloat16), "ctx").astype(jnp.float32),
        lax.psum(shares[4].astype(jnp.bfloat16), "ctx").astype(jnp.float32),
        lax.psum(shares[5].astype(jnp.bfloat16), "ctx").astype(jnp.float32),
        lax.psum(shares[6].astype(jnp.bfloat16), "ctx").astype(jnp.float32),
        lax.psum(shares[7].astype(jnp.bfloat16), "ctx").astype(jnp.float32),
        lax.psum(shares[8].astype(jnp.bfloat16), "ctx").astype(jnp.float32),
    )
    return (
        hidden_out,
        hidden_grad,
        owned[0],
        owned[1],
        owned[2],
        owned[3],
        owned[4],
        owned[5],
        owned[6],
        owned[7],
        owned[8],
    )


def solution(mesh):
    return jax.shard_map(
        per_device,
        mesh=mesh,
        in_specs=(
            P("fsdp", "ctx", None),
            P("fsdp"),
            P("fsdp", "ctx", None),
            P(None, "fsdp", "tp"),
            P(None, "tp", "fsdp"),
            P("tp", "fsdp"),
            P(None, "fsdp"),
            P(None, "fsdp"),
            P(None, "fsdp"),
            P(None, ("fsdp", "tp")),
            P(("fsdp", "tp")),
            P(("fsdp", "tp"), None),
        ),
        out_specs=(
            P("fsdp", "ctx", None),
            P("fsdp", "ctx", None),
            P(None, "fsdp", "tp"),
            P(None, "tp", "fsdp"),
            P("tp", "fsdp"),
            P(None, "fsdp"),
            P(None, "fsdp"),
            P(None, "fsdp"),
            P(None, ("fsdp", "tp")),
            P(("fsdp", "tp")),
            P(("fsdp", "tp"), None),
        ),
        check_vma=False,
    )
```

profile of v0, /device:TPU:0, one launch (start us, length us, event | category | flops | bytes accessed | tf_op | source)
XLA Modules:
  0.0 1103.8 jit_solution(3920871484078852565)
XLA Ops:
  8.7 14.8 %all_gather.34 = bf16[2,6,64]{1,0,2:T(2,128)(2,1)S(1)} all-gather(bf16[2,6,16]{1,0,2:T(2,128)(2,1)S(1)} %copy.57), channel_id=1, replica_groups=mesh['fsdp'=4,'ctx'=4,'tp'=2] {'fsdp'}, dimensions={2}, use_global_device_ids=true | all-gather | bytes 1920 | tf_op jit(solution)/shard_map/all_gather | solution.py:125
  24.0 24.4 %all_gather.35 = bf16[384,768]{0,1:T(8,128)(2,1)S(1)} all-gather(bf16[384,192]{0,1:T(8,128)(2,1)} %param.21), channel_id=1, replica_groups=mesh['fsdp'=4,'ctx'=4,'tp'=2] {'fsdp'}, dimensions={1}, use_global_device_ids=true | all-gather | bytes 737280 | tf_op jit(solution)/shard_map/all_gather | solution.py:126
  48.5 13.6 %all-gather.16.cloned.1.call-done = bf16[3,768,384]{2,1,0:T(8,128)(2,1)} async-done(((bf16[3,192,384]{2,1,0:T(8,128)(2,1)}), bf16[3,768,384]{2,1,0:T(8,128)(2,1)}) %all-gather.16.cloned.1.call-update) | async-done | bytes 1769488 | tf_op jit(solution)/shard_map/all_gather | solution.py:124
  62.1 4.1 fusion.18
  67.7 162.6 %while.24 = (s32[]{:T(128)}, bf16[4,256,384]{2,1,0:T(8,128)(2,1)S(1)}, f32[4,6,256]{2,1,0:T(8,128)S(1)}, bf16[4,2,256,384]{2,3,1,0:T(8,128)(2,1)}, s32[4]{0:T(12...) while((s32[]{:T(128)}, bf16[4,256,384]{2,1,0:T(8,128)(2,1)S(1)}, f32[4,6,256]{2,1,0:T(8,128)S(1)}, ...), condition=%wide.region_7.8_spmd, body=%wide.region_0.7_spmd.sunk | while | flops 414353920 | bytes 35844252 | solution.py:154
  70.8 30.0 %all-gather.22.cloned.1.call-done = bf16[1,2,1024,384]{2,3,1,0:T(8,128)(2,1)} async-done(((bf16[1,2,256,384]{2,3,1,0:T(8,128)(2,1)}), bf16[1,2,1024,384]{2,3,1,0:T(8,128)(2,1)}) %all-gather.22.cloned.1.call-update) | async-done | bytes 1572880 | tf_op jit(solution)/shard_map/while/body/eval_jaxpr/all_gather | solution.py:35
  110.8 31.1 %all-gather.22.cloned.1.call-done = bf16[1,2,1024,384]{2,3,1,0:T(8,128)(2,1)} async-done(((bf16[1,2,256,384]{2,3,1,0:T(8,128)(2,1)}), bf16[1,2,1024,384]{2,3,1,0:T(8,128)(2,1)}) %all-gather.22.cloned.1.call-update) | async-done | bytes 1572880 | tf_op jit(solution)/shard_map/while/body/eval_jaxpr/all_gather | solution.py:35
  151.9 30.8 %all-gather.22.cloned.1.call-done = bf16[1,2,1024,384]{2,3,1,0:T(8,128)(2,1)} async-done(((bf16[1,2,256,384]{2,3,1,0:T(8,128)(2,1)}), bf16[1,2,1024,384]{2,3,1,0:T(8,128)(2,1)}) %all-gather.22.cloned.1.call-update) | async-done | bytes 1572880 | tf_op jit(solution)/shard_map/while/body/eval_jaxpr/all_gather | solution.py:35
  192.7 30.8 %all-gather.22.cloned.1.call-done = bf16[1,2,1024,384]{2,3,1,0:T(8,128)(2,1)} async-done(((bf16[1,2,256,384]{2,3,1,0:T(8,128)(2,1)}), bf16[1,2,1024,384]{2,3,1,0:T(8,128)(2,1)}) %all-gather.22.cloned.1.call-update) | async-done | bytes 1572880 | tf_op jit(solution)/shard_map/while/body/eval_jaxpr/all_gather | solution.py:35
  230.4 2.7 fusion.62
  234.7 10.9 all-gather.2
  245.8 7.6 all-gather.3
  253.5 9.6 all-gather.4
  263.2 12.6 %all-gather.5 = bf16[4,1,384]{2,1,0:T(2,128)(2,1)S(1)} all-gather(bf16[1,1,384]{2,1,0:T(2,128)(2,1)S(1)} %reshape.402), channel_id=1, replica_groups=mesh['fsdp'=4,'ctx'=4,'tp'=2] {'fsdp'}, dimensions={0}, use_global_device_ids=true | all-gather | bytes 3840 | tf_op jit(solution)/shard_map/all_gather | solution.py:131
  275.9 2.9 fusion.47
  279.3 30.5 %all-gather.18.cloned.1.call-done = bf16[768,1536]{1,0:T(8,128)(2,1)} async-done(((bf16[768,384]{1,0:T(8,128)(2,1)}), bf16[768,1536]{1,0:T(8,128)(2,1)}) %all-gather.18.cloned.1.call-update) | async-done | bytes 2359312 | tf_op jit(solution)/shard_map/all_gather | solution.py:130
  309.7 19.6 %multiply_convert_fusion.3 = (bf16[1024,1536]{1,0:T(8,128)(2,1)}, f32[1024,1536]{1,0:T(8,128)}, f32[1024,1536]{1,0:T(8,128)}) fusion(f32[1536]{0:T(1024)S(1)} %reshape.404, bf16[768,1536]{1,0:T(8,128)(2,1)} %all-gather.18.cloned.1.call-done, f32[1024,768]{1,0:T(8,128)S(1)} %get-tuple-element.255, f32[768]{0:T(1024)S(1)} %get-tuple-element.199, ...), kind=kOutput, calls=%fused_computation.70 | convolution fusion | flops 2523660288 | bytes 21254144 | tf_op jit(solution)/shard_map/dot_general | solution.py:172
  329.3 31.3 %all-gather.20.cloned.1.call-done = bf16[1536,768]{1,0:T(8,128)(2,1)} async-done(((bf16[384,768]{1,0:T(8,128)(2,1)}), bf16[1536,768]{1,0:T(8,128)(2,1)}) %all-gather.20.cloned.1.call-update) | async-done | bytes 2359312 | tf_op jit(solution)/shard_map/all_gather | solution.py:132
  360.6 6.9 fusion.63
  368.5 21.3 %all-reduce.11.cloned.1.call-done = f32[1024,768]{1,0:T(8,128)} async-done(((f32[1024,768]{1,0:T(8,128)}), f32[1024,768]{1,0:T(8,128)}) %all-reduce.11.cloned.1.call-update) | async-done | bytes 3145744 | tf_op jit(solution)/shard_map/psum | solution.py:177
  389.7 3.0 fusion.45
  395.8 2.8 fusion.44
  401.5 4.5 fusion.40
  407.7 4.3 fusion.64
  412.1 6.1 convolution_convert_fusion.7
  418.2 4.4 copy.86
  422.6 14.0 %all-reduce.13.cloned.1.call-done = f32[1024,768]{1,0:T(8,128)} async-done(((f32[1024,768]{1,0:T(8,128)}), f32[1024,768]{1,0:T(8,128)}) %all-reduce.13.cloned.1.call-update) | async-done | bytes 3145744 | tf_op jit(solution)/shard_map/psum | solution.py:204
  436.6 3.7 multiply_reduce_fusion.5
  444.3 306.6 %while.25 = (s32[]{:T(128)}, bf16[4,256,384]{2,1,0:T(8,128)(2,1)}, bf16[4,2,256,384]{3,2,1,0:T(8,128)(2,1)}, bf16[4,2,256,384]{2,3,1,0:T(8,128)(2,1)}, s32[4]{0:...) while((s32[]{:T(128)}, bf16[4,256,384]{2,1,0:T(8,128)(2,1)}, ...), condition=%wide.region_24.25_spmd, body=%wide.region_19.24_spmd.sunk | while | flops 1028259328 | bytes 90409344 | solution.py:217
  444.6 2.0 constant_dynamic-slice_fusion.7
  449.1 30.3 %all-gather.24.cloned.1.call-done = bf16[1,2,1024,384]{2,3,1,0:T(8,128)(2,1)} async-done(((bf16[1,2,256,384]{2,3,1,0:T(8,128)(2,1)}), bf16[1,2,1024,384]{2,3,1,0:T(8,128)(2,1)}) %all-gather.24.cloned.1.call-update) | async-done | bytes 1572880 | tf_op jit(solution)/shard_map/while/body/eval_jaxpr/all_gather | solution.py:59
  493.3 26.9 %reduce-scatter.38.cloned.1.call-done = bf16[2,256,384]{1,2,0:T(8,128)(2,1)} async-done(((bf16[2,1024,384]{1,2,0:T(8,128)(2,1)}), bf16[2,256,384]{1,2,0:T(8,128)(2,1)}) %reduce-scatter.38.cloned.1.call-update) | async-done | bytes 393232 | tf_op jit(solution)/shard_map/while/body/eval_jaxpr/reduce_scatter | solution.py:103
  522.2 2.0 constant_dynamic-slice_fusion.7
  526.7 29.1 %all-gather.24.cloned.1.call-done = bf16[1,2,1024,384]{2,3,1,0:T(8,128)(2,1)} async-done(((bf16[1,2,256,384]{2,3,1,0:T(8,128)(2,1)}), bf16[1,2,1024,384]{2,3,1,0:T(8,128)(2,1)}) %all-gather.24.cloned.1.call-update) | async-done | bytes 1572880 | tf_op jit(solution)/shard_map/while/body/eval_jaxpr/all_gather | solution.py:59
  569.7 26.9 %reduce-scatter.38.cloned.1.call-done = bf16[2,256,384]{1,2,0:T(8,128)(2,1)} async-done(((bf16[2,1024,384]{1,2,0:T(8,128)(2,1)}), bf16[2,256,384]{1,2,0:T(8,128)(2,1)}) %reduce-scatter.38.cloned.1.call-update) | async-done | bytes 393232 | tf_op jit(solution)/shard_map/while/body/eval_jaxpr/reduce_scatter | solution.py:103
  598.6 2.0 constant_dynamic-slice_fusion.7
  603.2 28.8 %all-gather.24.cloned.1.call-done = bf16[1,2,1024,384]{2,3,1,0:T(8,128)(2,1)} async-done(((bf16[1,2,256,384]{2,3,1,0:T(8,128)(2,1)}), bf16[1,2,1024,384]{2,3,1,0:T(8,128)(2,1)}) %all-gather.24.cloned.1.call-update) | async-done | bytes 1572880 | tf_op jit(solution)/shard_map/while/body/eval_jaxpr/all_gather | solution.py:59
  645.9 26.9 %reduce-scatter.38.cloned.1.call-done = bf16[2,256,384]{1,2,0:T(8,128)(2,1)} async-done(((bf16[2,1024,384]{1,2,0:T(8,128)(2,1)}), bf16[2,256,384]{1,2,0:T(8,128)(2,1)}) %reduce-scatter.38.cloned.1.call-update) | async-done | bytes 393232 | tf_op jit(solution)/shard_map/while/body/eval_jaxpr/reduce_scatter | solution.py:103
  674.8 2.0 constant_dynamic-slice_fusion.7
  679.3 28.8 %all-gather.24.cloned.1.call-done = bf16[1,2,1024,384]{2,3,1,0:T(8,128)(2,1)} async-done(((bf16[1,2,256,384]{2,3,1,0:T(8,128)(2,1)}), bf16[1,2,1024,384]{2,3,1,0:T(8,128)(2,1)}) %all-gather.24.cloned.1.call-update) | async-done | bytes 1572880 | tf_op jit(solution)/shard_map/while/body/eval_jaxpr/all_gather | solution.py:59
  722.0 26.9 %reduce-scatter.38.cloned.1.call-done = bf16[2,256,384]{1,2,0:T(8,128)(2,1)} async-done(((bf16[2,1024,384]{1,2,0:T(8,128)(2,1)}), bf16[2,256,384]{1,2,0:T(8,128)(2,1)}) %reduce-scatter.38.cloned.1.call-update) | async-done | bytes 393232 | tf_op jit(solution)/shard_map/while/body/eval_jaxpr/reduce_scatter | solution.py:103
  751.7 5.4 fusion.23
  757.1 4.0 copy.76
  762.8 3.4 convolution_convert_fusion.9
  766.5 6.0 convolution_convert_fusion.6
  779.9 5.4 bitcast_convert_fusion.2
  785.3 16.9 %reduce-scatter.36.cloned.1.call-done = bf16[384,768]{1,0:T(8,128)(2,1)} async-done(((bf16[1536,768]{1,0:T(8,128)(2,1)}), bf16[384,768]{1,0:T(8,128)(2,1)}) %reduce-scatter.36.cloned.1.call-update) | async-done | bytes 589840
  802.2 2.1 copy.87
  804.3 38.1 %reduce-scatter.26.cloned.1.call-done = bf16[192,1152]{1,0:T(8,128)(2,1)} async-done(((bf16[768,1152]{1,0:T(8,128)(2,1)}), bf16[192,1152]{1,0:T(8,128)(2,1)}) %reduce-scatter.26.cloned.1.call-update) | async-done | bytes 442384
  842.4 2.1 reshape.410
  844.5 2.1 copy.77
  846.6 19.7 %reduce-scatter.22.cloned.1.call-done = bf16[384,192]{0,1:T(8,128)(2,1)} async-done(((bf16[384,768]{0,1:T(8,128)(2,1)}), bf16[384,192]{0,1:T(8,128)(2,1)}) %reduce-scatter.22.cloned.1.call-update) | async-done | bytes 147472 | tf_op jit(solution)/shard_map/reduce_scatter | solution.py:265
  866.4 48.7 %reduce-scatter.24.cloned.1.call-done = bf16[384,768]{1,0:T(8,128)(2,1)} async-done(((bf16[1536,768]{1,0:T(8,128)(2,1)}), bf16[384,768]{1,0:T(8,128)(2,1)}) %reduce-scatter.24.cloned.1.call-update) | async-done | bytes 589840 | tf_op jit(solution)/shard_map/reduce_scatter | solution.py:283
  916.3 9.9 all-reduce
  926.4 9.4 reduce-scatter.28.cloned.1.call-done
  936.6 18.9 %reduce-scatter.32.cloned.1.call-done = bf16[192,2]{1,0:T(8,128)(2,1)} async-done(((bf16[768,2]{1,0:T(8,128)(2,1)}), bf16[192,2]{1,0:T(8,128)(2,1)}) %reduce-scatter.32.cloned.1.call-update) | async-done | bytes 784
  956.3 19.6 %reduce-scatter.30.cloned.1.call-done = bf16[192,2]{1,0:T(8,128)(2,1)} async-done(((bf16[768,2]{1,0:T(8,128)(2,1)}), bf16[192,2]{1,0:T(8,128)(2,1)}) %reduce-scatter.30.cloned.1.call-update) | async-done | bytes 784
  976.8 18.9 %reduce-scatter.34.cloned.1.call-done = bf16[192,2]{1,0:T(8,128)(2,1)} async-done(((bf16[768,2]{1,0:T(8,128)(2,1)}), bf16[192,2]{1,0:T(8,128)(2,1)}) %reduce-scatter.34.cloned.1.call-update) | async-done | bytes 784
  996.6 10.0 all-reduce.1
  1009.5 7.6 all-reduce.15.cloned.1.call-done
  1017.1 3.0 add_convert_fusion.2
  1020.1 70.2 %all-reduce.17.cloned.1.call-done = (bf16[3,192,384]{1,2,0:T(8,128)(2,1)}, bf16[384,192]{0,1:T(8,128)(2,1)}, bf16[768,384]{1,0:T(8,128)(2,1)}, bf16[384,768]{1,0:T(8,128)(2,1)}) async-done(((bf16[3,192,384]{1,2,0:T(8,128)(2,1)}, bf16[384,192]{0,1:T(8,128)(2,1)}, bf16[768,384]{1,0:T(8,128)(2,1)}, bf16[384,768]{1,0:T(8,128)(2,1)}), (bf16[3,192,384]{1,2,0:T(8,128)(2,1)}, bf16[384,192]{0,1:T(8,128)(2,1)}, ...) | async-done | bytes 1769488 | tf_op jit(solution)/shard_map/psum | solution.py:288
  1090.3 2.2 convert_element_type.272
  1092.5 2.2 convert_element_type.275
  (469 shorter events, 149.5 us)
Async XLA Ops:
  7.2 54.9 %all-gather.16.cloned.1.call-start = ((), (), s32[]{:S(2)}) async-start(), calls=%async_computation.9 | async-start | bytes 2211840 | tf_op jit(solution)/shard_map/all_gather | solution.py:124
  48.4 182.0 %copy-start.8 = (bf16[384,768]{0,1:T(8,128)(2,1)}, bf16[384,768]{0,1:T(8,128)(2,1)S(1)}, u32[]{:S(2)}) copy-start(bf16[384,768]{0,1:T(8,128)(2,1)S(1)} %all_gather.35) | copy-start | bytes 1769476
  67.7 33.1 %all-gather.22.cloned.1.call-start = ((), (), s32[]{:S(2)}) async-start(), calls=%async_computation.25 | async-start | bytes 1966080 | tf_op jit(solution)/shard_map/while/body/eval_jaxpr/all_gather | solution.py:35
  107.7 34.3 %all-gather.22.cloned.1.call-start = ((), (), s32[]{:S(2)}) async-start(), calls=%async_computation.25 | async-start | bytes 1966080 | tf_op jit(solution)/shard_map/while/body/eval_jaxpr/all_gather | solution.py:35
  148.8 33.9 %all-gather.22.cloned.1.call-start = ((), (), s32[]{:S(2)}) async-start(), calls=%async_computation.25 | async-start | bytes 1966080 | tf_op jit(solution)/shard_map/while/body/eval_jaxpr/all_gather | solution.py:35
  189.5 33.9 %all-gather.22.cloned.1.call-start = ((), (), s32[]{:S(2)}) async-start(), calls=%async_computation.25 | async-start | bytes 1966080 | tf_op jit(solution)/shard_map/while/body/eval_jaxpr/all_gather | solution.py:35
  230.3 2.8 copy-start.7
  230.3 2.8 copy-start.16
  230.4 45.5 %all-reduce.9.cloned.1.call-start = ((), (), s32[]{:S(2)}) async-start(), calls=%async_computation.10 | async-start | bytes 6291456 | tf_op jit(solution)/shard_map/psum | solution.py:162
  233.1 12.6 %copy-start.22 = (bf16[2,192]{1,0:T(2,128)(2,1)S(1)}, bf16[2,192]{1,0:T(2,128)(2,1)}, u32[]{:S(2)}) copy-start(bf16[2,192]{1,0:T(2,128)(2,1)} %param.23) | copy-start | bytes 2308
  233.1 20.3 %copy-start.23 = (bf16[2,192]{1,0:T(2,128)(2,1)S(1)}, bf16[2,192]{1,0:T(2,128)(2,1)}, u32[]{:S(2)}) copy-start(bf16[2,192]{1,0:T(2,128)(2,1)} %param.24) | copy-start | bytes 2308
  233.1 30.1 %copy-start.24 = (bf16[384]{0:T(512)(128)(2,1)S(1)}, bf16[384]{0:T(512)(128)(2,1)}, u32[]{:S(2)}) copy-start(bf16[384]{0:T(512)(128)(2,1)} %param.26) | copy-start | bytes 2308
  233.2 76.5 %all-gather.18.cloned.1.call-start = ((), (), s32[]{:S(2)}) async-start(), calls=%async_computation.11 | async-start | bytes 2949120 | tf_op jit(solution)/shard_map/all_gather | solution.py:130
  233.9 126.7 %all-gather.20.cloned.1.call-start = ((), (), s32[]{:S(2)}) async-start(), calls=%async_computation.12 | async-start | bytes 2949120 | tf_op jit(solution)/shard_map/all_gather | solution.py:132
  234.7 155.0 %all-reduce.11.cloned.1.call-start = ((), (), s32[]{:S(2)}) async-start(), calls=%async_computation.13 | async-start | bytes 6291456 | tf_op jit(solution)/shard_map/psum | solution.py:177
  367.6 69.1 %all-reduce.13.cloned.1.call-start = ((), (), s32[]{:S(2)}) async-start(), calls=%async_computation.14 | async-start | bytes 6291456 | tf_op jit(solution)/shard_map/psum | solution.py:204
  389.7 10.9 slice-start.2
  394.2 6.4 slice-start.3
  395.8 4.8 slice-start
  395.8 4.8 slice-start.1
  398.6 2.9 copy-start.27
  400.6 5.5 copy-start.10
  401.5 6.2 copy-start.26
  406.0 1.7 copy-start.29
  441.8 2.5 copy-start.3
  442.2 2.1 copy-start.12
  444.5 36.4 %copy-start.13 = (bf16[4,256,384]{2,1,0:T(8,128)(2,1)}, bf16[4,256,384]{2,1,0:T(8,128)(2,1)S(1)}, u32[]{:S(2)}) copy-start(bf16[4,256,384]{2,1,0:T(8,128)(2,1)S(1)} %get-tuple-element.526) | copy-start | bytes 2359300 | tf_op jit(solution)/shard_map/while
  444.6 34.8 %all-gather.24.cloned.1.call-start = ((), (), s32[]{:S(2)}) async-start(), calls=%async_computation.26 | async-start | bytes 1966080 | tf_op jit(solution)/shard_map/while/body/eval_jaxpr/all_gather | solution.py:59
  446.6 73.5 %reduce-scatter.38.cloned.1.call-start = ((), (), s32[]{:S(2)}) async-start(), calls=%async_computation.27 | async-start | bytes 1966080 | tf_op jit(solution)/shard_map/while/body/eval_jaxpr/reduce_scatter | solution.py:103
  481.0 2.7 copy-start
  490.5 31.7 %copy-start.14 = (bf16[4,256,384]{2,1,0:T(8,128)(2,1)S(1)}, bf16[4,256,384]{2,1,0:T(8,128)(2,1)}, u32[]{:S(2)}) copy-start(bf16[4,256,384]{2,1,0:T(8,128)(2,1)} %copy-done.13) | copy-start | bytes 2359300 | tf_op jit(solution)/shard_map/while
  522.2 35.2 %copy-start.13 = (bf16[4,256,384]{2,1,0:T(8,128)(2,1)}, bf16[4,256,384]{2,1,0:T(8,128)(2,1)S(1)}, u32[]{:S(2)}) copy-start(bf16[4,256,384]{2,1,0:T(8,128)(2,1)S(1)} %get-tuple-element.526) | copy-start | bytes 2359300 | tf_op jit(solution)/shard_map/while
  522.2 33.7 %all-gather.24.cloned.1.call-start = ((), (), s32[]{:S(2)}) async-start(), calls=%async_computation.26 | async-start | bytes 1966080 | tf_op jit(solution)/shard_map/while/body/eval_jaxpr/all_gather | solution.py:59
  524.2 72.4 %reduce-scatter.38.cloned.1.call-start = ((), (), s32[]{:S(2)}) async-start(), calls=%async_computation.27 | async-start | bytes 1966080 | tf_op jit(solution)/shard_map/while/body/eval_jaxpr/reduce_scatter | solution.py:103
  557.5 2.7 copy-start
  566.9 31.7 %copy-start.14 = (bf16[4,256,384]{2,1,0:T(8,128)(2,1)S(1)}, bf16[4,256,384]{2,1,0:T(8,128)(2,1)}, u32[]{:S(2)}) copy-start(bf16[4,256,384]{2,1,0:T(8,128)(2,1)} %copy-done.13) | copy-start | bytes 2359300 | tf_op jit(solution)/shard_map/while
  598.6 34.8 %copy-start.13 = (bf16[4,256,384]{2,1,0:T(8,128)(2,1)}, bf16[4,256,384]{2,1,0:T(8,128)(2,1)S(1)}, u32[]{:S(2)}) copy-start(bf16[4,256,384]{2,1,0:T(8,128)(2,1)S(1)} %get-tuple-element.526) | copy-start | bytes 2359300 | tf_op jit(solution)/shard_map/while
  598.6 33.3 %all-gather.24.cloned.1.call-start = ((), (), s32[]{:S(2)}) async-start(), calls=%async_computation.26 | async-start | bytes 1966080 | tf_op jit(solution)/shard_map/while/body/eval_jaxpr/all_gather | solution.py:59
  600.7 72.1 %reduce-scatter.38.cloned.1.call-start = ((), (), s32[]{:S(2)}) async-start(), calls=%async_computation.27 | async-start | bytes 1966080 | tf_op jit(solution)/shard_map/while/body/eval_jaxpr/reduce_scatter | solution.py:103
  633.6 2.7 copy-start
  643.0 31.7 %copy-start.14 = (bf16[4,256,384]{2,1,0:T(8,128)(2,1)S(1)}, bf16[4,256,384]{2,1,0:T(8,128)(2,1)}, u32[]{:S(2)}) copy-start(bf16[4,256,384]{2,1,0:T(8,128)(2,1)} %copy-done.13) | copy-start | bytes 2359300 | tf_op jit(solution)/shard_map/while
  674.8 34.8 %copy-start.13 = (bf16[4,256,384]{2,1,0:T(8,128)(2,1)}, bf16[4,256,384]{2,1,0:T(8,128)(2,1)S(1)}, u32[]{:S(2)}) copy-start(bf16[4,256,384]{2,1,0:T(8,128)(2,1)S(1)} %get-tuple-element.526) | copy-start | bytes 2359300 | tf_op jit(solution)/shard_map/while
  674.8 33.3 %all-gather.24.cloned.1.call-start = ((), (), s32[]{:S(2)}) async-start(), calls=%async_computation.26 | async-start | bytes 1966080 | tf_op jit(solution)/shard_map/while/body/eval_jaxpr/all_gather | solution.py:59
  676.8 72.1 %reduce-scatter.38.cloned.1.call-start = ((), (), s32[]{:S(2)}) async-start(), calls=%async_computation.27 | async-start | bytes 1966080 | tf_op jit(solution)/shard_map/while/body/eval_jaxpr/reduce_scatter | solution.py:103
  709.7 2.7 copy-start
  719.2 31.7 %copy-start.14 = (bf16[4,256,384]{2,1,0:T(8,128)(2,1)S(1)}, bf16[4,256,384]{2,1,0:T(8,128)(2,1)}, u32[]{:S(2)}) copy-start(bf16[4,256,384]{2,1,0:T(8,128)(2,1)} %copy-done.13) | copy-start | bytes 2359300 | tf_op jit(solution)/shard_map/while
  750.9 51.3 %reduce-scatter.36.cloned.1.call-start = ((), (), s32[]{:S(2)}) async-start(), calls=%async_computation.23 | async-start | bytes 2949120
  751.6 90.7 %reduce-scatter.26.cloned.1.call-start = ((), (), s32[]{:S(2)}) async-start(), calls=%async_computation.18 | async-start | bytes 2211840
  761.2 1.7 copy-start.17
  762.8 3.8 copy-start.11
  762.8 103.6 %reduce-scatter.22.cloned.1.call-start = ((), (), s32[]{:S(2)}) async-start(), calls=%async_computation.16 | async-start | bytes 737280 | tf_op jit(solution)/shard_map/reduce_scatter | solution.py:265
  766.2 6.5 copy-start.20
  766.2 148.8 %reduce-scatter.24.cloned.1.call-start = ((), (), s32[]{:S(2)}) async-start(), calls=%async_computation.17 | async-start | bytes 2949120 | tf_op jit(solution)/shard_map/reduce_scatter | solution.py:283
  772.6 1.9 copy-start.15
  772.6 163.1 %reduce-scatter.28.cloned.1.call-start = ((), (), s32[]{:S(2)}) async-start(), calls=%async_computation.19 | async-start | bytes 20480
  777.0 178.5 %reduce-scatter.32.cloned.1.call-start = ((), (), s32[]{:S(2)}) async-start(), calls=%async_computation.21 | async-start | bytes 245760
  777.9 198.0 %reduce-scatter.30.cloned.1.call-start = ((), (), s32[]{:S(2)}) async-start(), calls=%async_computation.20 | async-start | bytes 245760
  778.9 216.8 %reduce-scatter.34.cloned.1.call-start = ((), (), s32[]{:S(2)}) async-start(), calls=%async_computation.22 | async-start | bytes 245760
  779.8 237.3 %all-reduce.15.cloned.1.call-start = ((), (), s32[]{:S(2)}) async-start(), calls=%async_computation.15 | async-start | bytes 3145728 | tf_op jit(solution)/shard_map/psum | solution.py:245
  785.2 129.9 %copy-start.28 = (u32[32]{0:T(128)S(1)}, u32[32]{0:T(128)}, u32[]{:S(2)}) copy-start(u32[32]{0:T(128)} %constant.143) | copy-start | bytes 388
  785.2 231.9 %copy-start.4 = (f32[1024,768]{1,0:T(8,128)S(1)}, f32[1024,768]{1,0:T(8,128)}, u32[]{:S(2)}) copy-start(f32[1024,768]{1,0:T(8,128)} %copy-done.3) | copy-start | bytes 9437188
  785.3 305.0 %all-reduce.17.cloned.1.call-start = ((), (), s32[]{:S(2)}) async-start(), calls=%async_computation.24 | async-start | bytes 3833856 | tf_op jit(solution)/shard_map/psum | solution.py:288
  1090.3 4.4 copy-start.18
  1090.3 5.5 copy-start.19
  (10 other events, 14.2 us)
Sparse Core Ops, SparseCore 0:
  9.6 52.4 all-gather.15
  71.1 29.6 all-gather.21
  111.0 30.8 all-gather.21
  151.8 30.8 all-gather.21
  192.6 30.8 all-gather.21
  233.3 23.1 all-reduce.8
  258.2 51.4 all-gather.17
  311.4 49.2 all-gather.19
  367.7 22.0 all-reduce.10
  412.2 24.3 all-reduce.12
  447.4 31.9 all-gather.23
  489.2 30.9 reduce-scatter.37
  525.0 30.8 all-gather.23
  565.6 30.9 reduce-scatter.37
  601.1 30.7 all-gather.23
  641.8 30.9 reduce-scatter.37
  677.2 30.7 all-gather.23
  717.9 30.9 reduce-scatter.37
  754.1 47.9 reduce-scatter.35
  804.5 37.8 reduce-scatter.25
  845.2 21.0 reduce-scatter.21
  868.7 46.3 reduce-scatter.23
  917.3 18.3 reduce-scatter.27
  937.9 17.4 reduce-scatter.31
  958.3 17.6 reduce-scatter.29
  978.1 17.5 reduce-scatter.33
  998.5 18.6 all-reduce.14
  1021.6 68.6 all-reduce.16
where the time goes:
time: 1110 us; the launch traced here: 1100 us
  waiting for transfers between devices  729 us (66%)
  matrix products  119 us (11%)
  blocking collectives  99.8 us (9%)
  local copies, waits for them, and re-layouts  86.6 us (8%)
  other arithmetic  50.7 us (5%)
  between operations  16 us (1%)
    unnamed x22, waiting for transfers between devices  125 us
    all_gather x4, waiting for transfers between devices, attend_slot(): gathered = lax.all_gather(key_value, 'ctx', axis=1, tiled=True)  123 us
    all_gather x4, waiting for transfers between devices, slot_grads(): gathered = lax.all_gather(key_value, 'ctx', axis=1, tiled=True)  117 us
    reduce_scatter x4, waiting for transfers between devices, slot_grads(): lax.psum_scatter(key_terms.astype(jnp.bfloat16), 'ctx', scatter_dimension...  108 us
    psum x1, waiting for transfers between devices, per_device(): lax.psum(shares[0].astype(jnp.bfloat16), 'ctx').astype(jnp.float32)  70.2 us
    reduce_scatter x1, waiting for transfers between devices, per_device(): lax.psum_scatter(grad_down.astype(jnp.bfloat16), 'fsdp', scatter_dimensio...  48.7 us
    unnamed x88, local copies, waits for them, and re-layouts  34.5 us
    all_gather x1, waiting for transfers between devices, per_device(): lax.all_gather(w_ffo, 'fsdp', axis=0, tiled=True)  31.3 us
  transfers between devices with their start and end apart: 28, of which 27 were waited for; matrix products, arithmetic and copies ran while one was open for 10% of the time, Pallas kernels for 0%

commit v1 on v0

--- a/solution.py
+++ b/solution.py
@@ -6,6 +6,18 @@
 epsilon = 1e-05
 masked_value = -1e30
 heads_together = 2
+
+
+def doubled_up(array, axis, dim):
+    ways, here, step = (lax.axis_size(axis), lax.axis_index(axis), array.shape[dim])
+    line, have = (array, 1)
+    while have < ways:
+        line = jnp.concatenate(
+            [line, lax.ppermute(line, axis, [(d, (d - have) % ways) for d in range(ways)])],
+            axis=dim,
+        )
+        have = 2 * have
+    return jnp.roll(line, here * step, axis=dim)
 
 
 def norm_rows(residual, gain_row, shift_row):
@@ -32,7 +44,7 @@
 
 
 def attend_slot(queries, key_value, length, score_scale, head_dim):
-    gathered = lax.all_gather(key_value, "ctx", axis=1, tiled=True)
+    gathered = doubled_up(key_value, "ctx", 1)
     seq_len = gathered.shape[1]
     key_mask = lax.iota(jnp.int32, seq_len) < length
     block_width = heads_together * head_dim

time: 1110 us -> 1110 us (level)
  waiting for transfers between devices: 729 us -> 687 us
  local copies, waits for them, and re-layouts: 86.6 us -> 107 us
  starting transfers between devices: 1.41 us -> 20.6 us
    all_gather x4 -> x0, waiting for transfers between devices: 123 us -> none  [attend_slot(): gathered = lax.all_gather(key_value, 'ctx', axis=1, tiled=True)]
    ppermute x0 -> x8, waiting for transfers between devices: none -> 77.1 us  [doubled_up(): lax.ppermute(line, axis, [(d, (d - have) % ways) for d in range(ways)])]
    while x32 -> x52, local copies, waits for them, and re-layouts: 0.07 us -> 21.1 us
    ppermute x0 -> x8, starting transfers between devices: none -> 19.3 us  [doubled_up(): lax.ppermute(line, axis, [(d, (d - have) % ways) for d in range(ways)])]
    unnamed x88 -> x84, local copies, waits for them, and re-layouts: 34.5 us -> 34.5 us
  transfers between devices with their start and end apart: 28 -> 32, of which waited for: 27 -> 31; matrix products, arithmetic and copies ran while one was open for 10% -> 11% of each run, Pallas kernels for 0% -> 0%
where the time goes in v1:
time: 1110 us; the launch traced here: 1100 us
  waiting for transfers between devices  687 us (62%)
  matrix products  120 us (11%)
  local copies, waits for them, and re-layouts  107 us (10%)
  blocking collectives  98.8 us (9%)
  other arithmetic  50.9 us (5%)
  starting transfers between devices  20.6 us (2%)
  between operations  16 us (1%)
    unnamed x22, waiting for transfers between devices  124 us
    all_gather x4, waiting for transfers between devices, slot_grads(): gathered = lax.all_gather(key_value, 'ctx', axis=1, tiled=True)  118 us
    reduce_scatter x4, waiting for transfers between devices, slot_grads(): lax.psum_scatter(key_terms.astype(jnp.bfloat16), 'ctx', scatter_dimension...  108 us
    ppermute x8, waiting for transfers between devices, doubled_up(): lax.ppermute(line, axis, [(d, (d - have) % ways) for d in range(ways)])  77.1 us
    psum x1, waiting for transfers between devices, per_device(): lax.psum(shares[0].astype(jnp.bfloat16), 'ctx').astype(jnp.float32)  70 us
    reduce_scatter x1, waiting for transfers between devices, per_device(): lax.psum_scatter(grad_down.astype(jnp.bfloat16), 'fsdp', scatter_dimensio...  48.5 us
    all_gather x1, waiting for transfers between devices, per_device(): lax.all_gather(w_in, 'fsdp', axis=1, tiled=True)  34.6 us
    unnamed x84, local copies, waits for them, and re-layouts  34.5 us
  transfers between devices with their start and end apart: 32, of which 31 were waited for; matrix products, arithmetic and copies ran while one was open for 11% of the time, Pallas kernels for 0%

profile of v1, /device:TPU:0, one launch (start us, length us, event | category | flops | bytes accessed | tf_op | source)
XLA Modules:
  0.0 1101.8 jit_solution(4061136415342956548)
XLA Ops:
  8.8 14.8 %all_gather.31 = bf16[2,6,64]{1,0,2:T(2,128)(2,1)S(1)} all-gather(bf16[2,6,16]{1,0,2:T(2,128)(2,1)S(1)} %copy.57), channel_id=1, replica_groups=mesh['fsdp'=4,'ctx'=4,'tp'=2] {'fsdp'}, dimensions={2}, use_global_device_ids=true | all-gather | bytes 1920 | tf_op jit(solution)/shard_map/all_gather | solution.py:137
  24.1 24.9 %all_gather.32 = bf16[384,768]{0,1:T(8,128)(2,1)} all-gather(bf16[384,192]{0,1:T(8,128)(2,1)} %param.21), channel_id=1, replica_groups=mesh['fsdp'=4,'ctx'=4,'tp'=2] {'fsdp'}, dimensions={1}, use_global_device_ids=true | all-gather | bytes 737280 | tf_op jit(solution)/shard_map/all_gather | solution.py:138
  49.0 13.1 %all-gather.12.cloned.1.call-done = bf16[3,768,384]{2,1,0:T(8,128)(2,1)} async-done(((bf16[3,192,384]{2,1,0:T(8,128)(2,1)}), bf16[3,768,384]{2,1,0:T(8,128)(2,1)}) %all-gather.12.cloned.1.call-update) | async-done | bytes 1769488 | tf_op jit(solution)/shard_map/all_gather | solution.py:136
  62.1 4.1 fusion.18
  67.7 156.7 %while.26 = (s32[]{:T(128)}, bf16[4,256,384]{2,1,0:T(8,128)(2,1)}, f32[4,6,256]{2,1,0:T(8,128)S(1)}, bf16[4,2,256,384]{2,3,1,0:T(8,128)(2,1)}, s32[4]{0:T(128)S(...) while((s32[]{:T(128)}, bf16[4,256,384]{2,1,0:T(8,128)(2,1)}, ...), condition=%wide.region_7.8_spmd, body=%wide.region_0.7_spmd.sunk | while | flops 415926816 | bytes 42136032 | solution.py:166
  69.5 2.4 collective-permute-start
  71.9 8.4 collective-permute-done
  84.1 14.8 %collective-permute-done.1 = bf16[2,512,384]{1,2,0:T(8,128)(2,1)S(1)} collective-permute-done((bf16[2,512,384]{1,2,0:T(8,128)(2,1)S(1)}, bf16[2,512,384]{1,2,0:T(8,128)(2,1)S(1)}, u32[]{:S(2)}, u32[]{:S(2)}) %collective-permute-start.1) | collective-permute-done | bytes 786464 | tf_op jit(solution)/shard_map/while/body/eval_jaxpr/ppermute | solution.py:16
  111.7 3.3 collective-permute-start
  115.0 6.5 collective-permute-done
  125.1 13.2 %collective-permute-done.1 = bf16[2,512,384]{1,2,0:T(8,128)(2,1)S(1)} collective-permute-done((bf16[2,512,384]{1,2,0:T(8,128)(2,1)S(1)}, bf16[2,512,384]{1,2,0:T(8,128)(2,1)S(1)}, u32[]{:S(2)}, u32[]{:S(2)}) %collective-permute-start.1) | collective-permute-done | bytes 786464 | tf_op jit(solution)/shard_map/while/body/eval_jaxpr/ppermute | solution.py:16
  151.2 3.5 collective-permute-start
  154.7 5.3 collective-permute-done
  163.2 11.8 %collective-permute-done.1 = bf16[2,512,384]{1,2,0:T(8,128)(2,1)S(1)} collective-permute-done((bf16[2,512,384]{1,2,0:T(8,128)(2,1)S(1)}, bf16[2,512,384]{1,2,0:T(8,128)(2,1)S(1)}, u32[]{:S(2)}, u32[]{:S(2)}) %collective-permute-start.1) | collective-permute-done | bytes 786464 | tf_op jit(solution)/shard_map/while/body/eval_jaxpr/ppermute | solution.py:16
  187.9 5.2 collective-permute-start
  193.1 5.3 collective-permute-done
  201.7 11.7 %collective-permute-done.1 = bf16[2,512,384]{1,2,0:T(8,128)(2,1)S(1)} collective-permute-done((bf16[2,512,384]{1,2,0:T(8,128)(2,1)S(1)}, bf16[2,512,384]{1,2,0:T(8,128)(2,1)S(1)}, u32[]{:S(2)}, u32[]{:S(2)}) %collective-permute-start.1) | collective-permute-done | bytes 786464 | tf_op jit(solution)/shard_map/while/body/eval_jaxpr/ppermute | solution.py:16
  224.4 4.3 fusion.62
  230.1 9.5 all-gather.1
  239.7 7.7 all-gather.2
  247.6 9.5 all-gather.3
  257.2 12.5 %all-gather.4 = bf16[4,1,384]{2,1,0:T(2,128)(2,1)S(1)} all-gather(bf16[1,1,384]{2,1,0:T(2,128)(2,1)S(1)} %reshape.439), channel_id=1, replica_groups=mesh['fsdp'=4,'ctx'=4,'tp'=2] {'fsdp'}, dimensions={0}, use_global_device_ids=true | all-gather | bytes 3840 | tf_op jit(solution)/shard_map/all_gather | solution.py:143
  269.7 2.8 fusion.47
  273.1 34.6 %all-gather.14.cloned.1.call-done = bf16[768,1536]{1,0:T(8,128)(2,1)} async-done(((bf16[768,384]{1,0:T(8,128)(2,1)}), bf16[768,1536]{1,0:T(8,128)(2,1)}) %all-gather.14.cloned.1.call-update) | async-done | bytes 2359312 | tf_op jit(solution)/shard_map/all_gather | solution.py:142
  307.7 19.5 %multiply_convert_fusion.3 = (bf16[1024,1536]{1,0:T(8,128)(2,1)}, f32[1024,1536]{1,0:T(8,128)}, f32[1024,1536]{1,0:T(8,128)}) fusion(f32[1536]{0:T(1024)S(1)} %reshape.441, bf16[768,1536]{1,0:T(8,128)(2,1)} %all-gather.14.cloned.1.call-done, f32[1024,768]{1,0:T(8,128)S(1)} %get-tuple-element.304, f32[768]{0:T(1024)S(1)} %get-tuple-element.246, ...), kind=kOutput, calls=%fused_computation.77 | convolution fusion | flops 2523660288 | bytes 21254144 | tf_op jit(solution)/shard_map/dot_general | solution.py:184
  327.3 31.2 %all-gather.16.cloned.1.call-done = bf16[1536,768]{1,0:T(8,128)(2,1)} async-done(((bf16[384,768]{1,0:T(8,128)(2,1)}), bf16[1536,768]{1,0:T(8,128)(2,1)}) %all-gather.16.cloned.1.call-update) | async-done | bytes 2359312 | tf_op jit(solution)/shard_map/all_gather | solution.py:144
  358.5 6.9 fusion.63
  366.3 21.3 %all-reduce.11.cloned.1.call-done = f32[1024,768]{1,0:T(8,128)} async-done(((f32[1024,768]{1,0:T(8,128)}), f32[1024,768]{1,0:T(8,128)}) %all-reduce.11.cloned.1.call-update) | async-done | bytes 3145744 | tf_op jit(solution)/shard_map/psum | solution.py:189
  387.6 3.0 fusion.45
  393.6 2.8 fusion.44
  399.3 4.5 fusion.40
  405.6 4.3 fusion.64
  409.9 6.1 convolution_convert_fusion.7
  416.1 4.4 copy.86
  420.4 14.0 %all-reduce.13.cloned.1.call-done = f32[1024,768]{1,0:T(8,128)} async-done(((f32[1024,768]{1,0:T(8,128)}), f32[1024,768]{1,0:T(8,128)}) %all-reduce.13.cloned.1.call-update) | async-done | bytes 3145744 | tf_op jit(solution)/shard_map/psum | solution.py:216
  434.5 3.7 multiply_reduce_fusion.5
  442.2 307.2 %while.27 = (s32[]{:T(128)}, bf16[4,256,384]{2,1,0:T(8,128)(2,1)}, bf16[4,2,256,384]{3,2,1,0:T(8,128)(2,1)}, bf16[4,2,256,384]{2,3,1,0:T(8,128)(2,1)}, s32[4]{0:...) while((s32[]{:T(128)}, bf16[4,256,384]{2,1,0:T(8,128)(2,1)}, ...), condition=%wide.region_24.25_spmd, body=%wide.region_19.24_spmd.sunk | while | flops 1028259328 | bytes 90409344 | solution.py:229
  447.0 30.3 %all-gather.18.cloned.1.call-done = bf16[1,2,1024,384]{2,3,1,0:T(8,128)(2,1)} async-done(((bf16[1,2,256,384]{2,3,1,0:T(8,128)(2,1)}), bf16[1,2,1024,384]{2,3,1,0:T(8,128)(2,1)}) %all-gather.18.cloned.1.call-update) | async-done | bytes 1572880 | tf_op jit(solution)/shard_map/while/body/eval_jaxpr/all_gather | solution.py:71
  491.2 26.9 %reduce-scatter.38.cloned.1.call-done = bf16[2,256,384]{1,2,0:T(8,128)(2,1)} async-done(((bf16[2,1024,384]{1,2,0:T(8,128)(2,1)}), bf16[2,256,384]{1,2,0:T(8,128)(2,1)}) %reduce-scatter.38.cloned.1.call-update) | async-done | bytes 393232 | tf_op jit(solution)/shard_map/while/body/eval_jaxpr/reduce_scatter | solution.py:115
  524.6 29.1 %all-gather.18.cloned.1.call-done = bf16[1,2,1024,384]{2,3,1,0:T(8,128)(2,1)} async-done(((bf16[1,2,256,384]{2,3,1,0:T(8,128)(2,1)}), bf16[1,2,1024,384]{2,3,1,0:T(8,128)(2,1)}) %all-gather.18.cloned.1.call-update) | async-done | bytes 1572880 | tf_op jit(solution)/shard_map/while/body/eval_jaxpr/all_gather | solution.py:71
  567.6 26.9 %reduce-scatter.38.cloned.1.call-done = bf16[2,256,384]{1,2,0:T(8,128)(2,1)} async-done(((bf16[2,1024,384]{1,2,0:T(8,128)(2,1)}), bf16[2,256,384]{1,2,0:T(8,128)(2,1)}) %reduce-scatter.38.cloned.1.call-update) | async-done | bytes 393232 | tf_op jit(solution)/shard_map/while/body/eval_jaxpr/reduce_scatter | solution.py:115
  601.0 29.1 %all-gather.18.cloned.1.call-done = bf16[1,2,1024,384]{2,3,1,0:T(8,128)(2,1)} async-done(((bf16[1,2,256,384]{2,3,1,0:T(8,128)(2,1)}), bf16[1,2,1024,384]{2,3,1,0:T(8,128)(2,1)}) %all-gather.18.cloned.1.call-update) | async-done | bytes 1572880 | tf_op jit(solution)/shard_map/while/body/eval_jaxpr/all_gather | solution.py:71
  644.0 26.9 %reduce-scatter.38.cloned.1.call-done = bf16[2,256,384]{1,2,0:T(8,128)(2,1)} async-done(((bf16[2,1024,384]{1,2,0:T(8,128)(2,1)}), bf16[2,256,384]{1,2,0:T(8,128)(2,1)}) %reduce-scatter.38.cloned.1.call-update) | async-done | bytes 393232 | tf_op jit(solution)/shard_map/while/body/eval_jaxpr/reduce_scatter | solution.py:115
  677.5 29.1 %all-gather.18.cloned.1.call-done = bf16[1,2,1024,384]{2,3,1,0:T(8,128)(2,1)} async-done(((bf16[1,2,256,384]{2,3,1,0:T(8,128)(2,1)}), bf16[1,2,1024,384]{2,3,1,0:T(8,128)(2,1)}) %all-gather.18.cloned.1.call-update) | async-done | bytes 1572880 | tf_op jit(solution)/shard_map/while/body/eval_jaxpr/all_gather | solution.py:71
  720.4 26.9 %reduce-scatter.38.cloned.1.call-done = bf16[2,256,384]{1,2,0:T(8,128)(2,1)} async-done(((bf16[2,1024,384]{1,2,0:T(8,128)(2,1)}), bf16[2,256,384]{1,2,0:T(8,128)(2,1)}) %reduce-scatter.38.cloned.1.call-update) | async-done | bytes 393232 | tf_op jit(solution)/shard_map/while/body/eval_jaxpr/reduce_scatter | solution.py:115
  750.0 5.4 fusion.23
  755.4 4.0 copy.76
  761.1 3.4 convolution_convert_fusion.9
  764.8 6.0 convolution_convert_fusion.6
  778.1 5.4 bitcast_convert_fusion.2
  783.6 16.8 %reduce-scatter.36.cloned.1.call-done = bf16[384,768]{1,0:T(8,128)(2,1)} async-done(((bf16[1536,768]{1,0:T(8,128)(2,1)}), bf16[384,768]{1,0:T(8,128)(2,1)}) %reduce-scatter.36.cloned.1.call-update) | async-done | bytes 589840
  802.5 38.1 %reduce-scatter.26.cloned.1.call-done = bf16[192,1152]{1,0:T(8,128)(2,1)} async-done(((bf16[768,1152]{1,0:T(8,128)(2,1)}), bf16[192,1152]{1,0:T(8,128)(2,1)}) %reduce-scatter.26.cloned.1.call-update) | async-done | bytes 442384
  844.8 19.6 %reduce-scatter.22.cloned.1.call-done = bf16[384,192]{0,1:T(8,128)(2,1)} async-done(((bf16[384,768]{0,1:T(8,128)(2,1)}), bf16[384,192]{0,1:T(8,128)(2,1)}) %reduce-scatter.22.cloned.1.call-update) | async-done | bytes 147472 | tf_op jit(solution)/shard_map/reduce_scatter | solution.py:277
  864.4 48.5 %reduce-scatter.24.cloned.1.call-done = bf16[384,768]{1,0:T(8,128)(2,1)} async-done(((bf16[1536,768]{1,0:T(8,128)(2,1)}), bf16[384,768]{1,0:T(8,128)(2,1)}) %reduce-scatter.24.cloned.1.call-update) | async-done | bytes 589840 | tf_op jit(solution)/shard_map/reduce_scatter | solution.py:295
  914.2 9.9 all-reduce
  924.2 9.3 reduce-scatter.28.cloned.1.call-done
  934.4 18.9 %reduce-scatter.32.cloned.1.call-done = bf16[192,2]{1,0:T(8,128)(2,1)} async-done(((bf16[768,2]{1,0:T(8,128)(2,1)}), bf16[192,2]{1,0:T(8,128)(2,1)}) %reduce-scatter.32.cloned.1.call-update) | async-done | bytes 784
  954.2 19.6 %reduce-scatter.30.cloned.1.call-done = bf16[192,2]{1,0:T(8,128)(2,1)} async-done(((bf16[768,2]{1,0:T(8,128)(2,1)}), bf16[192,2]{1,0:T(8,128)(2,1)}) %reduce-scatter.30.cloned.1.call-update) | async-done | bytes 784
  974.6 19.0 %reduce-scatter.34.cloned.1.call-done = bf16[192,2]{1,0:T(8,128)(2,1)} async-done(((bf16[768,2]{1,0:T(8,128)(2,1)}), bf16[192,2]{1,0:T(8,128)(2,1)}) %reduce-scatter.34.cloned.1.call-update) | async-done | bytes 784
  994.5 10.0 all-reduce.1
  1007.5 7.8 all-reduce.15.cloned.1.call-done
  1015.2 3.0 add_convert_fusion.2
  1018.2 70.0 %all-reduce.17.cloned.1.call-done = (bf16[3,192,384]{1,2,0:T(8,128)(2,1)}, bf16[384,192]{0,1:T(8,128)(2,1)}, bf16[768,384]{1,0:T(8,128)(2,1)}, bf16[384,768]{1,0:T(8,128)(2,1)}) async-done(((bf16[3,192,384]{1,2,0:T(8,128)(2,1)}, bf16[384,192]{0,1:T(8,128)(2,1)}, bf16[768,384]{1,0:T(8,128)(2,1)}, bf16[384,768]{1,0:T(8,128)(2,1)}), (bf16[3,192,384]{1,2,0:T(8,128)(2,1)}, bf16[384,192]{0,1:T(8,128)(2,1)}, ...) | async-done | bytes 1769488 | tf_op jit(solution)/shard_map/psum | solution.py:300
  1088.3 2.2 convert_element_type.284
  (493 shorter events, 191.3 us)
Async XLA Ops:
  7.2 54.9 %all-gather.12.cloned.1.call-start = ((), (), s32[]{:S(2)}) async-start(), calls=%async_computation.9 | async-start | bytes 2211840 | tf_op jit(solution)/shard_map/all_gather | solution.py:136
  7.9 261.8 %all-reduce.9.cloned.1.call-start = ((), (), s32[]{:S(2)}) async-start(), calls=%async_computation.10 | async-start | bytes 6291456 | tf_op jit(solution)/shard_map/psum | solution.py:174
  69.5 10.8 collective-permute-start
  80.4 18.4 %collective-permute-start.1 = (bf16[2,512,384]{1,2,0:T(8,128)(2,1)S(1)}, bf16[2,512,384]{1,2,0:T(8,128)(2,1)S(1)}, u32[]{:S(2)}, u32[]{:S(2)}) collective-permute-start(bf16[2,512,384]{1,2,0:T(8,128)(2,1)S(1)} %pad_maximum_fusion.14), channel_id=1, source_target_pairs={{0,4},{2,6},{4,0},{6,2},{1,5},{3,7},{5,1},{7,3},{8,12},{10,14},{12... | collective-permute-start | bytes 2359304 | tf_op jit(solution)/shard_map/while/body/eval_jaxpr/ppermute | solution.py:16
  111.7 9.8 collective-permute-start
  121.6 16.7 %collective-permute-start.1 = (bf16[2,512,384]{1,2,0:T(8,128)(2,1)S(1)}, bf16[2,512,384]{1,2,0:T(8,128)(2,1)S(1)}, u32[]{:S(2)}, u32[]{:S(2)}) collective-permute-start(bf16[2,512,384]{1,2,0:T(8,128)(2,1)S(1)} %pad_maximum_fusion.14), channel_id=1, source_target_pairs={{0,4},{2,6},{4,0},{6,2},{1,5},{3,7},{5,1},{7,3},{8,12},{10,14},{12... | collective-permute-start | bytes 2359304 | tf_op jit(solution)/shard_map/while/body/eval_jaxpr/ppermute | solution.py:16
  151.2 8.8 collective-permute-start
  160.1 14.9 %collective-permute-start.1 = (bf16[2,512,384]{1,2,0:T(8,128)(2,1)S(1)}, bf16[2,512,384]{1,2,0:T(8,128)(2,1)S(1)}, u32[]{:S(2)}, u32[]{:S(2)}) collective-permute-start(bf16[2,512,384]{1,2,0:T(8,128)(2,1)S(1)} %pad_maximum_fusion.14), channel_id=1, source_target_pairs={{0,4},{2,6},{4,0},{6,2},{1,5},{3,7},{5,1},{7,3},{8,12},{10,14},{12... | collective-permute-start | bytes 2359304 | tf_op jit(solution)/shard_map/while/body/eval_jaxpr/ppermute | solution.py:16
  187.9 10.5 collective-permute-start
  198.5 14.9 %collective-permute-start.1 = (bf16[2,512,384]{1,2,0:T(8,128)(2,1)S(1)}, bf16[2,512,384]{1,2,0:T(8,128)(2,1)S(1)}, u32[]{:S(2)}, u32[]{:S(2)}) collective-permute-start(bf16[2,512,384]{1,2,0:T(8,128)(2,1)S(1)} %pad_maximum_fusion.14), channel_id=1, source_target_pairs={{0,4},{2,6},{4,0},{6,2},{1,5},{3,7},{5,1},{7,3},{8,12},{10,14},{12... | collective-permute-start | bytes 2359304 | tf_op jit(solution)/shard_map/while/body/eval_jaxpr/ppermute | solution.py:16
  224.4 4.3 copy-start.7
  228.7 11.0 copy-start.20
  228.7 18.8 %copy-start.21 = (bf16[2,192]{1,0:T(2,128)(2,1)S(1)}, bf16[2,192]{1,0:T(2,128)(2,1)}, u32[]{:S(2)}) copy-start(bf16[2,192]{1,0:T(2,128)(2,1)} %param.24) | copy-start | bytes 2308
  228.7 28.4 %copy-start.22 = (bf16[384]{0:T(512)(128)(2,1)S(1)}, bf16[384]{0:T(512)(128)(2,1)}, u32[]{:S(2)}) copy-start(bf16[384]{0:T(512)(128)(2,1)} %param.26) | copy-start | bytes 2308
  228.8 79.0 %all-gather.14.cloned.1.call-start = ((), (), s32[]{:S(2)}) async-start(), calls=%async_computation.11 | async-start | bytes 2949120 | tf_op jit(solution)/shard_map/all_gather | solution.py:142
  229.5 129.0 %all-gather.16.cloned.1.call-start = ((), (), s32[]{:S(2)}) async-start(), calls=%async_computation.12 | async-start | bytes 2949120 | tf_op jit(solution)/shard_map/all_gather | solution.py:144
  230.1 157.5 %all-reduce.11.cloned.1.call-start = ((), (), s32[]{:S(2)}) async-start(), calls=%async_computation.13 | async-start | bytes 6291456 | tf_op jit(solution)/shard_map/psum | solution.py:189
  365.4 69.1 %all-reduce.13.cloned.1.call-start = ((), (), s32[]{:S(2)}) async-start(), calls=%async_computation.14 | async-start | bytes 6291456 | tf_op jit(solution)/shard_map/psum | solution.py:216
  387.6 10.9 slice-start.2
  392.0 6.4 slice-start.3
  393.6 4.8 slice-start
  393.6 4.8 slice-start.1
  396.4 2.9 copy-start.25
  398.4 5.5 copy-start.9
  399.3 6.2 copy-start.24
  439.7 2.5 copy-start.3
  440.0 2.1 copy-start.11
  442.4 36.4 %copy-start.12 = (bf16[4,256,384]{2,1,0:T(8,128)(2,1)}, bf16[4,256,384]{2,1,0:T(8,128)(2,1)S(1)}, u32[]{:S(2)}) copy-start(bf16[4,256,384]{2,1,0:T(8,128)(2,1)S(1)} %get-tuple-element.603) | copy-start | bytes 2359300 | tf_op jit(solution)/shard_map/while
  442.4 34.9 %all-gather.18.cloned.1.call-start = ((), (), s32[]{:S(2)}) async-start(), calls=%async_computation.25 | async-start | bytes 1966080 | tf_op jit(solution)/shard_map/while/body/eval_jaxpr/all_gather | solution.py:71
  444.5 73.6 %reduce-scatter.38.cloned.1.call-start = ((), (), s32[]{:S(2)}) async-start(), calls=%async_computation.26 | async-start | bytes 1966080 | tf_op jit(solution)/shard_map/while/body/eval_jaxpr/reduce_scatter | solution.py:115
  478.9 2.7 copy-start
  488.3 31.7 %copy-start.13 = (bf16[4,256,384]{2,1,0:T(8,128)(2,1)S(1)}, bf16[4,256,384]{2,1,0:T(8,128)(2,1)}, u32[]{:S(2)}) copy-start(bf16[4,256,384]{2,1,0:T(8,128)(2,1)} %copy-done.12) | copy-start | bytes 2359300 | tf_op jit(solution)/shard_map/while
  520.0 35.1 %copy-start.12 = (bf16[4,256,384]{2,1,0:T(8,128)(2,1)}, bf16[4,256,384]{2,1,0:T(8,128)(2,1)S(1)}, u32[]{:S(2)}) copy-start(bf16[4,256,384]{2,1,0:T(8,128)(2,1)S(1)} %get-tuple-element.603) | copy-start | bytes 2359300 | tf_op jit(solution)/shard_map/while
  520.0 33.6 %all-gather.18.cloned.1.call-start = ((), (), s32[]{:S(2)}) async-start(), calls=%async_computation.25 | async-start | bytes 1966080 | tf_op jit(solution)/shard_map/while/body/eval_jaxpr/all_gather | solution.py:71
  522.1 72.4 %reduce-scatter.38.cloned.1.call-start = ((), (), s32[]{:S(2)}) async-start(), calls=%async_computation.26 | async-start | bytes 1966080 | tf_op jit(solution)/shard_map/while/body/eval_jaxpr/reduce_scatter | solution.py:115
  555.3 2.7 copy-start
  564.8 31.7 %copy-start.13 = (bf16[4,256,384]{2,1,0:T(8,128)(2,1)S(1)}, bf16[4,256,384]{2,1,0:T(8,128)(2,1)}, u32[]{:S(2)}) copy-start(bf16[4,256,384]{2,1,0:T(8,128)(2,1)} %copy-done.12) | copy-start | bytes 2359300 | tf_op jit(solution)/shard_map/while
  596.5 35.1 %copy-start.12 = (bf16[4,256,384]{2,1,0:T(8,128)(2,1)}, bf16[4,256,384]{2,1,0:T(8,128)(2,1)S(1)}, u32[]{:S(2)}) copy-start(bf16[4,256,384]{2,1,0:T(8,128)(2,1)S(1)} %get-tuple-element.603) | copy-start | bytes 2359300 | tf_op jit(solution)/shard_map/while
  596.5 33.6 %all-gather.18.cloned.1.call-start = ((), (), s32[]{:S(2)}) async-start(), calls=%async_computation.25 | async-start | bytes 1966080 | tf_op jit(solution)/shard_map/while/body/eval_jaxpr/all_gather | solution.py:71
  598.5 72.4 %reduce-scatter.38.cloned.1.call-start = ((), (), s32[]{:S(2)}) async-start(), calls=%async_computation.26 | async-start | bytes 1966080 | tf_op jit(solution)/shard_map/while/body/eval_jaxpr/reduce_scatter | solution.py:115
  631.7 2.7 copy-start
  641.2 31.7 %copy-start.13 = (bf16[4,256,384]{2,1,0:T(8,128)(2,1)S(1)}, bf16[4,256,384]{2,1,0:T(8,128)(2,1)}, u32[]{:S(2)}) copy-start(bf16[4,256,384]{2,1,0:T(8,128)(2,1)} %copy-done.12) | copy-start | bytes 2359300 | tf_op jit(solution)/shard_map/while
  672.9 35.1 %copy-start.12 = (bf16[4,256,384]{2,1,0:T(8,128)(2,1)}, bf16[4,256,384]{2,1,0:T(8,128)(2,1)S(1)}, u32[]{:S(2)}) copy-start(bf16[4,256,384]{2,1,0:T(8,128)(2,1)S(1)} %get-tuple-element.603) | copy-start | bytes 2359300 | tf_op jit(solution)/shard_map/while
  672.9 33.6 %all-gather.18.cloned.1.call-start = ((), (), s32[]{:S(2)}) async-start(), calls=%async_computation.25 | async-start | bytes 1966080 | tf_op jit(solution)/shard_map/while/body/eval_jaxpr/all_gather | solution.py:71
  674.9 72.4 %reduce-scatter.38.cloned.1.call-start = ((), (), s32[]{:S(2)}) async-start(), calls=%async_computation.26 | async-start | bytes 1966080 | tf_op jit(solution)/shard_map/while/body/eval_jaxpr/reduce_scatter | solution.py:115
  708.2 2.7 copy-start
  717.6 31.7 %copy-start.13 = (bf16[4,256,384]{2,1,0:T(8,128)(2,1)S(1)}, bf16[4,256,384]{2,1,0:T(8,128)(2,1)}, u32[]{:S(2)}) copy-start(bf16[4,256,384]{2,1,0:T(8,128)(2,1)} %copy-done.12) | copy-start | bytes 2359300 | tf_op jit(solution)/shard_map/while
  749.4 51.0 %reduce-scatter.36.cloned.1.call-start = ((), (), s32[]{:S(2)}) async-start(), calls=%async_computation.23 | async-start | bytes 2949120
  749.9 90.6 %reduce-scatter.26.cloned.1.call-start = ((), (), s32[]{:S(2)}) async-start(), calls=%async_computation.18 | async-start | bytes 2211840
  761.0 3.8 copy-start.10
  761.0 103.3 %reduce-scatter.22.cloned.1.call-start = ((), (), s32[]{:S(2)}) async-start(), calls=%async_computation.16 | async-start | bytes 737280 | tf_op jit(solution)/shard_map/reduce_scatter | solution.py:277
  764.5 6.4 copy-start.18
  764.5 148.4 %reduce-scatter.24.cloned.1.call-start = ((), (), s32[]{:S(2)}) async-start(), calls=%async_computation.17 | async-start | bytes 2949120 | tf_op jit(solution)/shard_map/reduce_scatter | solution.py:295
  770.8 1.9 copy-start.14
  770.9 162.7 %reduce-scatter.28.cloned.1.call-start = ((), (), s32[]{:S(2)}) async-start(), calls=%async_computation.19 | async-start | bytes 20480
  775.2 178.1 %reduce-scatter.32.cloned.1.call-start = ((), (), s32[]{:S(2)}) async-start(), calls=%async_computation.21 | async-start | bytes 245760
  776.2 197.6 %reduce-scatter.30.cloned.1.call-start = ((), (), s32[]{:S(2)}) async-start(), calls=%async_computation.20 | async-start | bytes 245760
  777.1 216.5 %reduce-scatter.34.cloned.1.call-start = ((), (), s32[]{:S(2)}) async-start(), calls=%async_computation.22 | async-start | bytes 245760
  778.1 237.2 %all-reduce.15.cloned.1.call-start = ((), (), s32[]{:S(2)}) async-start(), calls=%async_computation.15 | async-start | bytes 3145728 | tf_op jit(solution)/shard_map/psum | solution.py:257
  783.5 129.5 %copy-start.26 = (u32[32]{0:T(128)S(1)}, u32[32]{0:T(128)}, u32[]{:S(2)}) copy-start(u32[32]{0:T(128)} %constant.210) | copy-start | bytes 388
  783.5 231.7 %copy-start.4 = (f32[1024,768]{1,0:T(8,128)S(1)}, f32[1024,768]{1,0:T(8,128)}, u32[]{:S(2)}) copy-start(f32[1024,768]{1,0:T(8,128)} %copy-done.3) | copy-start | bytes 9437188
  783.5 304.7 %all-reduce.17.cloned.1.call-start = ((), (), s32[]{:S(2)}) async-start(), calls=%async_computation.24 | async-start | bytes 3833856 | tf_op jit(solution)/shard_map/psum | solution.py:300
  1088.2 4.4 copy-start.16
  1088.3 5.5 copy-start.17
  (12 other events, 17.4 us)
Sparse Core Ops, SparseCore 0:
  9.6 52.4 all-gather.11
  228.9 25.5 all-reduce.8
  256.2 51.4 all-gather.13
  309.2 49.1 all-gather.15
  365.5 22.0 all-reduce.10
  410.0 24.3 all-reduce.12
  445.2 31.9 all-gather.17
  487.1 30.9 reduce-scatter.37
  522.8 30.7 all-gather.17
  563.5 30.9 reduce-scatter.37
  599.3 30.7 all-gather.17
  639.9 30.9 reduce-scatter.37
  675.7 30.7 all-gather.17
  716.4 30.9 reduce-scatter.37
  752.3 47.9 reduce-scatter.35
  802.6 37.8 reduce-scatter.25
  843.2 21.0 reduce-scatter.21
  866.5 46.3 reduce-scatter.23
  915.1 18.3 reduce-scatter.27
  935.8 17.4 reduce-scatter.31
  956.1 17.5 reduce-scatter.29
  976.1 17.4 reduce-scatter.33
  996.6 18.6 all-reduce.14
  1019.6 68.6 all-reduce.16
